TPU v7x, 256 devices: a whole 4x4x8 slice. The times are simulated.
256 devices in a mesh: grid: 8 (over x_lo, y), dom: 32 (over z, x_hi, core).
Axes of the slice: x: 4 (x_hi: 2, x_lo: 2; x = x_hi * 2 + x_lo), y: 4, z: 8, core: 2. Of those that a mesh axis runs over, the one named last changes fastest.
Arguments:
- state_field: float32 [8, 64, 8, 16384], P('grid', 'dom'), may hold values from -6 to 6
- level_vectors: int32 [8, 4], P('grid'), may hold values from 2 to 5, as said below
- combine_weights: int32 [8], P('grid'), may hold values from -2 to 2, as said below
- diffusion: float32 [6], replicated, may hold values from 0.05 to 0.08
- courant: float32 [6], replicated, may hold values from -0.3 to 0.3
Outputs:
- combined_field: float32 [8, 64, 8, 16384], P('grid', 'dom')
Inputs may be any that keep to these rules, and one draw needn't show every extreme that they name: `level_vectors`: each row holds 2, 3, 4, 5 in some order. `combine_weights`: never zero.
All inputs are finite; a program needn't handle non-finite values.
Results may differ from a plain program's by a relative error of at most 0.0003.
Values sent between devices are 32-bit elements; how exact they have to be, the bound alone decides.
No kernel may reach another device: no remote copies, remote signals or barrier semaphores. Data moves between devices by JAX's collectives and lax.ppermute only.
A program may use at most 128 MiB of HBM per device.

v0:
```python
import jax
import jax.numpy as jnp
from jax import lax
from jax.sharding import PartitionSpec as P

LOW = 2


def with_halo(x, sides, width):
    for axis, dim in sides:
        peers, length = (lax.axis_size(axis), x.shape[dim])
        up = [(i, (i + 1) % peers) for i in range(peers)]
        down = [(j, i) for i, j in up]
        last = lax.slice_in_dim(x, length - width, length, axis=dim)
        initial = lax.slice_in_dim(x, 0, width, axis=dim)
        before = lax.ppermute(last, axis, up)
        after = lax.ppermute(initial, axis, down)
        x = jnp.concatenate([before, x, after], axis=dim)
    return x


def from_everyone(x, axis):
    copies = jnp.broadcast_to(x, (lax.axis_size(axis), *x.shape))
    return lax.all_to_all(copies, axis, split_axis=0, concat_axis=0, tiled=True)


def taken_together(x, axis):
    everything = from_everyone(x, axis)
    return jnp.sum(everything, axis=0)


def spacings(length, orientation):
    ladder = [2**exponent for exponent in range(length.bit_length() - 1)]
    return ladder if orientation < 0 else ladder[::-1]


def digit_table(count, stride, length):
    return jnp.arange(count, dtype=jnp.int32) // stride % length


def flat_forward(values, stride, length, distance):
    digit = digit_table(values.shape[-1], stride, length)
    wrapped = jnp.roll(values, (length - distance) * stride, -1)
    plain = jnp.roll(values, -distance * stride, -1)
    return jnp.where(digit >= length - distance, wrapped, plain)


def flat_backward(values, stride, length, distance):
    digit = digit_table(values.shape[-1], stride, length)
    wrapped = jnp.roll(values, -(length - distance) * stride, -1)
    plain = jnp.roll(values, distance * stride, -1)
    return jnp.where(digit < distance, wrapped, plain)


def flat_level(values, stride, length, spacing, orientation):
    digit = digit_table(values.shape[-1], stride, length)
    lower = flat_backward(values, stride, length, spacing)
    upper = flat_forward(values, stride, length, spacing)
    active = digit % (2 * spacing) == spacing
    return jnp.where(active, values + orientation * 0.5 * (lower + upper), values)


def flat_sweep(values, layout, orientation):
    for stride, length in layout:
        for spacing in spacings(length, orientation):
            values = flat_level(values, stride, length, spacing, orientation)
    return values


def stencil_numbers(level_row, diffusion, courant):
    matches = (level_row[:, None] == (LOW + jnp.arange(4, dtype=jnp.int32))[None, :]).astype(
        jnp.float32
    )
    local_diff = jnp.sum(diffusion[2:, None] * matches, axis=0)
    local_cour = jnp.sum(courant[2:, None] * matches, axis=0)
    return (
        jnp.concatenate([diffusion[:2], local_diff]),
        jnp.concatenate([courant[:2], local_cour]),
    )


def subspace_map(level_row):
    side_len = 2**LOW
    entries = side_len**4
    flat_ids = jnp.arange(entries, dtype=jnp.int32)
    target = jnp.zeros((entries,), jnp.int32)
    for physical in range(4):
        digits = flat_ids // side_len ** (3 - physical) % side_len
        stored = level_row[physical] - LOW
        target = target + digits * jnp.power(side_len, 3 - stored).astype(jnp.int32)
    return (flat_ids[:, None] == target[None, :]).astype(jnp.float32)


def fine_layout(local_len):
    side_len = 2**LOW
    return [
        (local_len // side_len, side_len),
        (32 * side_len * side_len, 2 * side_len),
        (8 * side_len, 4 * side_len),
        (1, 8 * side_len),
    ]


def advance_rows(extended, diff_num, cour_num):
    center = extended[1:-1]
    forward_rows = extended[2:]
    backward_rows = extended[:-2]
    update = diff_num[0] * (forward_rows + backward_rows - 2.0 * center) - 0.5 * cour_num[0] * (
        forward_rows - backward_rows
    )
    forward = jnp.roll(center, -1, 1)
    backward = jnp.roll(center, 1, 1)
    update = (
        update
        + diff_num[1] * (forward + backward - 2.0 * center)
        - 0.5 * cour_num[1] * (forward - backward)
    )
    for offset, (stride, length) in enumerate(fine_layout(center.shape[-1])):
        forward = flat_forward(center, stride, length, 1)
        backward = flat_backward(center, stride, length, 1)
        update = (
            update
            + diff_num[2 + offset] * (forward + backward - 2.0 * center)
            - 0.5 * cour_num[2 + offset] * (forward - backward)
        )
    return center + update


def coarse_selector(fine_cols):
    side_len = 2**LOW
    coarse_ids = jnp.arange(side_len**3, dtype=jnp.int32)
    first = coarse_ids // (side_len * side_len)
    middle = coarse_ids // side_len % side_len
    last = coarse_ids % side_len
    target = 2 * first * 32 * side_len * side_len + 4 * middle * 8 * side_len + 8 * last
    fine_ids = jnp.arange(fine_cols, dtype=jnp.int32)
    return (fine_ids[:, None] == target[None, :]).astype(jnp.float32)


def linear_spread(ratio):
    side_len = 2**LOW
    fine_ids = jnp.arange(ratio * side_len, dtype=jnp.int32)
    coarse_ids = jnp.arange(side_len, dtype=jnp.int32)
    gap = (fine_ids[None, :] - ratio * coarse_ids[:, None]) % (ratio * side_len)
    reach = jnp.minimum(gap, ratio * side_len - gap).astype(jnp.float32)
    return jnp.maximum(1.0 - reach / float(ratio), 0.0)


def spread_table(fine_cols):
    table = jnp.einsum("ad,be,cf->abcdef", linear_spread(2), linear_spread(4), linear_spread(8))
    return table.reshape(-1, fine_cols)


def local(state_field, level_vectors, combine_weights, diffusion, courant):
    values = state_field[0]
    row_count = values.shape[0]
    second_len = values.shape[1]
    local_len = values.shape[2]
    side_len = 2**LOW
    fine_cols = local_len // side_len
    diff_num, cour_num = stencil_numbers(level_vectors[0], diffusion, courant)
    extended = with_halo(values, (("dom", 0),), 2)
    for repeat in range(2):
        extended = advance_rows(extended, diff_num, cour_num)
    values = extended
    coarse_layout = [
        (side_len**3, side_len),
        (side_len**2, side_len),
        (side_len, side_len),
        (1, side_len),
    ]
    selector = coarse_selector(fine_cols)
    coarse = jnp.dot(
        values.reshape(row_count * second_len * side_len, fine_cols),
        selector,
        precision=lax.Precision.HIGHEST,
    )
    coarse = coarse.reshape(row_count, second_len * side_len**4)
    coarse = flat_sweep(coarse, coarse_layout, -1.0)
    mapping = subspace_map(level_vectors[0])
    shared = coarse.reshape(row_count * second_len, side_len**4)
    weighted = combine_weights[0].astype(jnp.float32) * jnp.dot(
        shared, mapping, precision=lax.Precision.HIGHEST
    )
    combined = taken_together(weighted, "grid")
    returned = jnp.dot(combined, mapping.T, precision=lax.Precision.HIGHEST)
    change = returned.reshape(row_count, -1) - coarse
    change = flat_sweep(change, coarse_layout, 1.0)
    spread = jnp.dot(
        change.reshape(row_count * second_len * side_len, side_len**3),
        spread_table(fine_cols),
        precision=lax.Precision.HIGHEST,
    )
    result = values + spread.reshape(row_count, second_len, local_len)
    return result.reshape(1, row_count, second_len, local_len)


def solution(mesh):
    placed = (P("grid", "dom", None, None), P("grid", None), P("grid"), P(), P())
    return jax.shard_map(
        local, mesh=mesh, in_specs=placed, out_specs=P("grid", "dom", None, None), check_vma=False
    )
```

profile of v0, /device:TPU:2, one launch (start us, length us, event | category | flops | bytes accessed | tf_op | source)
XLA Modules:
  0.0 137.3 jit_solution(3913293820259624696)
XLA Ops:
  0.0 6.9 %collective-permute-start.1 = (f32[2,8,16384]{2,1,0:T(8,128)}, f32[2,8,16384]{2,1,0:T(8,128)S(1)}, u32[]{:S(2)}, u32[]{:S(2)}) collective-permute-start(f32[2,8,16384]{2,1,0:T(8,128)} %bitcast.724), channel_id=1, source_target_pairs={{1,0},{2,1},{3,2},{4,3},{5,4},{6,5},{7,6},{8,7},{9,8},{10,9},{11,1... | collective-permute-start | bytes 3145736 | tf_op jit(solution)/shard_map/ppermute | solution.py:17
  7.6 1.4 %fusion.349 = (f32[1]{0:T(128)}, f32[1]{0:T(128)}) fusion(f32[6]{0:T(128)} %param.9), kind=kLoop, calls=%fused_computation.738 | loop fusion | bytes 16 | tf_op jit(solution)/shard_map/slice | solution.py:108
  9.7 1.3 fusion.348
  18.2 1.5 %fusion.347 = (s32[1,1]{1,0:T(1,128)}, s32[1,1]{1,0:T(1,128)}, s32[1,1]{1,0:T(1,128)}, s32[1,1]{1,0:T(1,128)}) fusion(s32[1,4]{1,0:T(1,128)} %param.6), kind=kLoop, calls=%fused_computation.736 | loop fusion | bytes 32 | tf_op jit(solution)/shard_map/slice | solution.py:89
  45.9 2.6 %multiply_bitcast_fusion = f32[4,4,4,8,16,32]{5,4,3,2,1,0:T(8,128)} fusion(f32[4,32]{1,0:T(4,128)S(1)} %fusion.252, f32[4,16,4,8]{1,3,0,2:T(8,128)S(1)} %broadcast_multiply_fusion), kind=kLoop, calls=%fused_computation | loop fusion | flops 262144 | bytes 1057280 | tf_op jit(solution)/shard_map/ad,be,cf->abcdef/transpose | solution.py:150
  50.8 2.1 %fusion.281 = (f32[4,8,16353]{2,1,0:T(8,128)S(1)}, f32[4,8,16353]{2,1,0:T(8,128)}) fusion(f32[6,8,16384]{2,1,0:T(8,128)S(1)} %pad_maximum_fusion), kind=kLoop, calls=%fused_computation.670 | loop fusion | bytes 8372736 | tf_op jit(solution)/shard_map/jit(_roll_static)/slice | solution.py:50
  52.9 2.7 %fusion.282 = (f32[4,8,16383]{2,1,0:T(8,128)}, f32[4,8,16383]{2,1,0:T(8,128)}) fusion(f32[6,8,16384]{2,1,0:T(8,128)S(1)} %pad_maximum_fusion), kind=kLoop, calls=%fused_computation.671 | loop fusion | bytes 8388096 | tf_op jit(solution)/shard_map/jit(_roll_static)/slice | solution.py:51
  55.5 2.5 %fusion.279 = (f32[4,8,15904]{2,1,0:T(8,128)}, f32[4,8,15904]{2,1,0:T(8,128)}) fusion(f32[6,8,16384]{2,1,0:T(8,128)S(1)} %pad_maximum_fusion), kind=kLoop, calls=%fused_computation.668 | loop fusion | bytes 8142848 | tf_op jit(solution)/shard_map/jit(_roll_static)/slice | solution.py:50
  58.1 2.2 %fusion.278 = (f32[4,8,15872]{2,1,0:T(8,128)}, f32[4,8,15872]{2,1,0:T(8,128)}) fusion(f32[6,8,16384]{2,1,0:T(8,128)S(1)} %pad_maximum_fusion), kind=kLoop, calls=%fused_computation.667 | loop fusion | bytes 8126464 | tf_op jit(solution)/shard_map/jit(_roll_static)/slice | solution.py:51
  60.3 1.9 %fusion.276 = (f32[4,8,12800]{2,1,0:T(8,128)}, f32[4,8,12800]{2,1,0:T(8,128)}) fusion(f32[6,8,16384]{2,1,0:T(8,128)S(1)} %pad_maximum_fusion), kind=kLoop, calls=%fused_computation.665 | loop fusion | bytes 6553600 | tf_op jit(solution)/shard_map/jit(_roll_static)/slice | solution.py:50
  62.2 2.0 %fusion.274 = (f32[4,8,12288]{2,1,0:T(8,128)}, f32[4,8,12288]{2,1,0:T(8,128)}) fusion(f32[6,8,16384]{2,1,0:T(8,128)S(1)} %pad_maximum_fusion), kind=kLoop, calls=%fused_computation.663 | loop fusion | bytes 6291456 | tf_op jit(solution)/shard_map/jit(_roll_static)/slice | solution.py:43
  64.2 1.1 fusion.275
  66.1 1.1 fusion.273
  67.2 19.8 %subtract_add_fusion = f32[4,8,16384]{2,1,0:T(8,128)S(1)} fusion(f32[2,8,16384]{2,1,0:T(8,128)} %copy-done.2, f32[2,8,16384]{2,1,0:T(8,128)} %bitcast.725, f32[2,8,16384]{2,1,0:T(8,128)} %copy-done.1, f32[4,8,16383]{2,1,0:T(8,128)} %get-tuple-element.78, f32[4,8,16353]{2,1,0:T(8,128)} %get-tuple-element.76, f32[4,8,16383]{2,1,0:T(8,128)} %get-tuple-element.77, ...), kind=kLoop, calls=%fused_computation.45 | loop fusion | flops 45613056 | bytes 40722480 | tf_op jit(solution)/shard_map/add | solution.py:126
  89.6 9.6 %subtract_add_fusion.1 = f32[2,8,16384]{2,1,0:T(8,128)S(1)} fusion(f32[2,8,16383]{2,1,0:T(8,128)S(1)} %get-tuple-element.108, f32[2,8,1]{2,1,0:T(8,128)S(1)} %get-tuple-element.110, f32[2,8,31]{2,1,0:T(8,128)S(1)} %get-tuple-element.104, f32[2,8,16353]{2,1,0:T(8,128)S(1)} %get-tuple-element.106, f32[2,8,1]{2,1,0:T(8,128)S(1)} %get-tuple-element.109, ...), kind=kLoop, calls=%fused_computation.75 | loop fusion | flops 17039360 | bytes 21069872 | tf_op jit(solution)/shard_map/add | solution.py:126
  99.9 1.6 %fusion.27 = f32[64,64]{1,0:T(8,128)S(1)} fusion(f32[64,4096]{1,0:T(8,128)S(1)} %reshape.581, s32[64]{0:T(128)} %fusion.266), kind=kOutput, calls=%fused_computation.61 | convolution fusion | flops 201588736 | bytes 1065216 | tf_op jit(solution)/shard_map/dot_general | solution.py:173
  106.2 5.9 %all-to-all-start = ((f32[8,16,256]{2,1,0:T(8,128)}), f32[8,16,256]{2,1,0:T(8,128)S(1)}, u32[]{:S(2)}, u32[]{:S(2)}) async-start(f32[8,16,256]{2,1,0:T(8,128)} %broadcast_in_dim.582), calls=%async_computation | async-start | bytes 262144 | tf_op jit(solution)/shard_map/all_to_all | solution.py:24
  112.1 3.5 %reshape.586 = f32[64,4096]{1,0:T(8,128)S(1)} reshape(f32[4,4,4,8,16,32]{5,4,3,2,1,0:T(8,128)} %multiply_bitcast_fusion) | data formatting | bytes 2097152 | tf_op jit(solution)/shard_map/reshape | solution.py:151
  125.9 1.4 %concatenate.585 = f32[64,64]{1,0:T(8,128)} reshape(f32[2,2048]{1,0:T(2,128)} %get-tuple-element.28) | data formatting | bytes 32768 | tf_op jit(solution)/shard_map/jit(_roll_static)/concatenate | solution.py:50
  127.3 1.4 %concatenate.587 = f32[64,64]{1,0:T(8,128)} reshape(f32[2,2048]{1,0:T(2,128)} %get-tuple-element.27) | data formatting | bytes 32768 | tf_op jit(solution)/shard_map/jit(_roll_static)/concatenate | solution.py:51
  128.7 1.4 %concatenate.589 = f32[64,64]{1,0:T(8,128)} reshape(f32[2,2048]{1,0:T(2,128)} %get-tuple-element.30) | data formatting | bytes 32768 | tf_op jit(solution)/shard_map/jit(_roll_static)/concatenate | solution.py:43
  130.1 1.4 %concatenate.591 = f32[64,64]{1,0:T(8,128)} reshape(f32[2,2048]{1,0:T(2,128)} %get-tuple-element.29) | data formatting | bytes 32768 | tf_op jit(solution)/shard_map/jit(_roll_static)/concatenate | solution.py:44
  131.5 1.4 %concatenate.581 = f32[64,64]{1,0:T(8,128)} reshape(f32[2,2048]{1,0:T(2,128)} %get-tuple-element.111) | data formatting | bytes 32768 | tf_op jit(solution)/shard_map/jit(_roll_static)/concatenate | solution.py:50
  133.6 1.1 add_select_fusion.5
  (331 shorter events, 51.1 us)
Async XLA Ops:
  0.0 48.5 %collective-permute-start = (f32[2,8,16384]{2,1,0:T(8,128)}, f32[2,8,16384]{2,1,0:T(8,128)S(1)}, u32[]{:S(2)}, u32[]{:S(2)}) collective-permute-start(f32[2,8,16384]{2,1,0:T(8,128)} %bitcast.723), channel_id=1, source_target_pairs={{0,1},{1,2},{2,3},{3,4},{4,5},{5,6},{6,7},{7,8},{8,9},{9,10},{10,1... | collective-permute-start | bytes 3145736 | tf_op jit(solution)/shard_map/ppermute | solution.py:16
  0.0 48.5 %collective-permute-start.1 = (f32[2,8,16384]{2,1,0:T(8,128)}, f32[2,8,16384]{2,1,0:T(8,128)S(1)}, u32[]{:S(2)}, u32[]{:S(2)}) collective-permute-start(f32[2,8,16384]{2,1,0:T(8,128)} %bitcast.724), channel_id=1, source_target_pairs={{1,0},{2,1},{3,2},{4,3},{5,4},{6,5},{7,6},{8,7},{9,8},{10,9},{11,1... | collective-permute-start | bytes 3145736 | tf_op jit(solution)/shard_map/ppermute | solution.py:17
  99.7 5.3 %copy-start.26 = (pred[8,256]{1,0:T(8,128)(4,1)S(1)}, pred[8,256]{1,0:T(8,128)(4,1)}, u32[]{:S(2)}) copy-start(pred[8,256]{1,0:T(8,128)(4,1)} %get-tuple-element.253) | copy-start | bytes 6148
  99.7 5.3 %copy-start.27 = (pred[8,256]{1,0:T(8,128)(4,1)S(1)}, pred[8,256]{1,0:T(8,128)(4,1)}, u32[]{:S(2)}) copy-start(pred[8,256]{1,0:T(8,128)(4,1)} %get-tuple-element.254) | copy-start | bytes 6148
  99.7 5.3 %copy-start.28 = (pred[8,256]{1,0:T(8,128)(4,1)S(1)}, pred[8,256]{1,0:T(8,128)(4,1)}, u32[]{:S(2)}) copy-start(pred[8,256]{1,0:T(8,128)(4,1)} %get-tuple-element.255) | copy-start | bytes 6148
  99.7 5.3 %copy-start.29 = (pred[8,256]{1,0:T(8,128)(4,1)S(1)}, pred[8,256]{1,0:T(8,128)(4,1)}, u32[]{:S(2)}) copy-start(pred[8,256]{1,0:T(8,128)(4,1)} %get-tuple-element.256) | copy-start | bytes 6148
  99.7 5.3 %copy-start.30 = (pred[8,256]{1,0:T(8,128)(4,1)S(1)}, pred[8,256]{1,0:T(8,128)(4,1)}, u32[]{:S(2)}) copy-start(pred[8,256]{1,0:T(8,128)(4,1)} %get-tuple-element.257) | copy-start | bytes 6148
  99.7 5.3 %copy-start.31 = (pred[8,256]{1,0:T(8,128)(4,1)S(1)}, pred[8,256]{1,0:T(8,128)(4,1)}, u32[]{:S(2)}) copy-start(pred[8,256]{1,0:T(8,128)(4,1)} %get-tuple-element.258) | copy-start | bytes 6148
  99.8 5.3 %copy-start.32 = (pred[8,256]{1,0:T(8,128)(4,1)S(1)}, pred[8,256]{1,0:T(8,128)(4,1)}, u32[]{:S(2)}) copy-start(pred[8,256]{1,0:T(8,128)(4,1)} %get-tuple-element.259) | copy-start | bytes 6148
  99.8 5.3 %copy-start.33 = (pred[8,256]{1,0:T(8,128)(4,1)S(1)}, pred[8,256]{1,0:T(8,128)(4,1)}, u32[]{:S(2)}) copy-start(pred[8,256]{1,0:T(8,128)(4,1)} %get-tuple-element.260) | copy-start | bytes 6148
  99.8 5.3 %copy-start.34 = (pred[8,256]{1,0:T(8,128)(4,1)S(1)}, pred[8,256]{1,0:T(8,128)(4,1)}, u32[]{:S(2)}) copy-start(pred[8,256]{1,0:T(8,128)(4,1)} %get-tuple-element.261) | copy-start | bytes 6148
  99.8 5.3 %copy-start.35 = (pred[8,256]{1,0:T(8,128)(4,1)S(1)}, pred[8,256]{1,0:T(8,128)(4,1)}, u32[]{:S(2)}) copy-start(pred[8,256]{1,0:T(8,128)(4,1)} %get-tuple-element.262) | copy-start | bytes 6148
  99.8 5.3 %copy-start.36 = (pred[8,256]{1,0:T(8,128)(4,1)S(1)}, pred[8,256]{1,0:T(8,128)(4,1)}, u32[]{:S(2)}) copy-start(pred[8,256]{1,0:T(8,128)(4,1)} %get-tuple-element.263) | copy-start | bytes 6148
  99.8 5.3 %copy-start.37 = (pred[8,256]{1,0:T(8,128)(4,1)S(1)}, pred[8,256]{1,0:T(8,128)(4,1)}, u32[]{:S(2)}) copy-start(pred[8,256]{1,0:T(8,128)(4,1)} %get-tuple-element.264) | copy-start | bytes 6148
  99.8 5.3 %copy-start.38 = (pred[8,256]{1,0:T(8,128)(4,1)S(1)}, pred[8,256]{1,0:T(8,128)(4,1)}, u32[]{:S(2)}) copy-start(pred[8,256]{1,0:T(8,128)(4,1)} %get-tuple-element.265) | copy-start | bytes 6148
  99.8 5.3 %copy-start.39 = (pred[8,256]{1,0:T(8,128)(4,1)S(1)}, pred[8,256]{1,0:T(8,128)(4,1)}, u32[]{:S(2)}) copy-start(pred[8,256]{1,0:T(8,128)(4,1)} %get-tuple-element.266) | copy-start | bytes 6148
  99.8 5.3 %copy-start.40 = (pred[8,256]{1,0:T(8,128)(4,1)S(1)}, pred[8,256]{1,0:T(8,128)(4,1)}, u32[]{:S(2)}) copy-start(pred[8,256]{1,0:T(8,128)(4,1)} %get-tuple-element.267) | copy-start | bytes 6148
  99.8 5.3 %copy-start.41 = (pred[8,256]{1,0:T(8,128)(4,1)S(1)}, pred[8,256]{1,0:T(8,128)(4,1)}, u32[]{:S(2)}) copy-start(pred[8,256]{1,0:T(8,128)(4,1)} %get-tuple-element.268) | copy-start | bytes 6148
  99.9 5.3 %copy-start.42 = (pred[8,256]{1,0:T(8,128)(4,1)S(1)}, pred[8,256]{1,0:T(8,128)(4,1)}, u32[]{:S(2)}) copy-start(pred[8,256]{1,0:T(8,128)(4,1)} %get-tuple-element.269) | copy-start | bytes 6148
  99.9 5.3 %copy-start.43 = (pred[8,256]{1,0:T(8,128)(4,1)S(1)}, pred[8,256]{1,0:T(8,128)(4,1)}, u32[]{:S(2)}) copy-start(pred[8,256]{1,0:T(8,128)(4,1)} %get-tuple-element.270) | copy-start | bytes 6148
  99.9 5.3 %copy-start.44 = (pred[8,256]{1,0:T(8,128)(4,1)S(1)}, pred[8,256]{1,0:T(8,128)(4,1)}, u32[]{:S(2)}) copy-start(pred[8,256]{1,0:T(8,128)(4,1)} %get-tuple-element.271) | copy-start | bytes 6148
  106.2 12.3 %all-to-all-start = ((f32[8,16,256]{2,1,0:T(8,128)}), f32[8,16,256]{2,1,0:T(8,128)S(1)}, u32[]{:S(2)}, u32[]{:S(2)}) async-start(f32[8,16,256]{2,1,0:T(8,128)} %broadcast_in_dim.582), calls=%async_computation | async-start | bytes 262144 | tf_op jit(solution)/shard_map/all_to_all | solution.py:24
  112.1 6.6 %copy-start.15 = (pred[2048]{0:T(1024)(128)(4,1)S(1)}, pred[2048]{0:T(1024)(128)(4,1)}, u32[]{:S(2)}) copy-start(pred[2048]{0:T(1024)(128)(4,1)} %get-tuple-element.277) | copy-start | bytes 6148
  112.1 6.6 %copy-start.16 = (pred[2048]{0:T(1024)(128)(4,1)S(1)}, pred[2048]{0:T(1024)(128)(4,1)}, u32[]{:S(2)}) copy-start(pred[2048]{0:T(1024)(128)(4,1)} %get-tuple-element.278) | copy-start | bytes 6148
  (30 other events, 95.7 us)
where the time goes:
time: 138 us; the launch traced here: 137 us
  other arithmetic  64.4 us (47%)
  local copies, waits for them, and re-layouts  48.8 us (35%)
  starting transfers between devices  12.8 us (9%)
  between operations  8.3 us (6%)
  matrix products  3.06 us (2%)
    add x2, other arithmetic, advance_rows(): return center + update  29.4 us
    lt x20, other arithmetic, flat_backward(): return jnp.where(digit < distance, wrapped, plain)  11 us
    eq x16, other arithmetic, flat_level(): active = digit % (2 * spacing) == spacing  8.54 us
    slice x10, local copies, waits for them, and re-layouts, flat_backward(): wrapped = jnp.roll(values, -(length - distance) * stride, -1)  7.54 us
    ppermute x1, starting transfers between devices, with_halo(): after = lax.ppermute(initial, axis, down)  6.86 us
    slice x13, local copies, waits for them, and re-layouts, flat_backward(): plain = jnp.roll(values, distance * stride, -1)  6.29 us
    all_to_all x1, starting transfers between devices, from_everyone(): return lax.all_to_all(copies, axis, split_axis=0, concat_axis=0, tiled=True)  5.93 us
    slice x26, local copies, waits for them, and re-layouts, flat_forward(): wrapped = jnp.roll(values, (length - distance) * stride, -1)  5.42 us
  transfers between devices with their start and end apart: 3, of which 0 were waited for; matrix products, arithmetic and copies ran while one was open for 30% of the time, Pallas kernels for 0%

commit v1 on v0

v1 whole, which is shorter than its diff:
```python
import jax
import jax.numpy as jnp
from jax import lax
from jax.experimental import pallas as pl
from jax.experimental.pallas import tpu as pltpu
from jax.sharding import PartitionSpec as P

AXES = ("grid", "dom")
VMEM = pltpu.VMEM
SMEM = pltpu.SMEM
F32 = jnp.float32
BF16 = jnp.bfloat16
LANES = 128
COLS = 16384


def roll(x, shift, axis):
    return pltpu.roll(x, shift, axis)


def numbers(level_ref, diff_ref, cour_ref):
    kappa = [diff_ref[0], diff_ref[1]]
    sigma = [cour_ref[0], cour_ref[1]]
    for j in range(4):
        k, s = F32(0.0), F32(0.0)
        for p in range(4):
            hit = level_ref[0, p] == 2 + j
            k = jnp.where(hit, diff_ref[2 + p], k)
            s = jnp.where(hit, cour_ref[2 + p], s)
        kappa.append(k)
        sigma.append(s)
    fwd = [k - 0.5 * s for k, s in zip(kappa, sigma)]
    bwd = [k + 0.5 * s for k, s in zip(kappa, sigma)]
    centre = 1.0 - 2.0 * (kappa[0] + kappa[1] + kappa[2] + kappa[3] + kappa[4] + kappa[5])
    return fwd, bwd, centre


def parity():
    return lax.axis_index("dom") % 2


def sides(fwd, bwd, p):
    off = jnp.where(p == 0, bwd[0], fwd[0])
    core = jnp.where(p == 0, fwd[0], bwd[0])
    return off, core


def at(i2, d3, c4):
    start = (i2 * 32 + d3 * 4 + c4) * LANES
    return pl.ds(pl.multiple_of(start, LANES), LANES)


def stencil(load, emit, i2, nums):
    fwd, bwd, centre = nums
    lane = lax.broadcasted_iota(jnp.int32, (8, LANES), 1)
    inner = lane % 32
    not_top, not_low = lane < 96, lane >= 32
    not_last, not_first = inner < 31, inner > 0
    above, below = (i2 + 1) % 4, (i2 + 3) % 4
    for d3 in range(8):
        v = [load(i2, d3, c) for c in range(4)]
        ahead = [roll(x, 96, 1) for x in v]
        behind = [roll(x, 32, 1) for x in v]
        for c in range(4):
            x = v[c]
            total = centre * x
            total += fwd[1] * roll(x, 7, 0) + bwd[1] * roll(x, 1, 0)
            total += fwd[2] * load(above, d3, c) + bwd[2] * load(below, d3, c)
            total += fwd[3] * load(i2, (d3 + 1) % 8, c) + bwd[3] * load(i2, (d3 + 7) % 8, c)
            total += fwd[4] * jnp.where(not_top, ahead[c], ahead[(c + 1) % 4])
            total += bwd[4] * jnp.where(not_low, behind[c], behind[(c + 3) % 4])
            total += fwd[5] * jnp.where(not_last, roll(x, 127, 1), roll(x, 31, 1))
            total += bwd[5] * jnp.where(not_first, roll(x, 1, 1), roll(x, 97, 1))
            emit(i2, d3, c, total)


def spots():
    for v in range(2):
        for g in range(4):
            for j in range(8):
                i2 = v * 2 + g // 2
                i3 = (g % 2) * 2 + j // 4
                yield v, g, j, i2, i3, j % 4


def pack(load):
    lane = lax.broadcasted_iota(jnp.int32, (8, LANES), 1)
    code = lane // 32 * 8 + lane % 8
    out = [None, None]
    for v, g, j, i2, i3, i4 in spots():
        x = load(i2, 2 * i3, i4)
        shift = 32 * g + j
        x = roll(x, shift, 1) if shift else x
        out[v] = x if out[v] is None else jnp.where(code == 8 * g + j, x, out[v])
    return jnp.concatenate(out, axis=1)


def first_kernel(u_ref, level_ref, diff_ref, cour_ref, z_ref, near_ref, far_ref):
    nums = numbers(level_ref, diff_ref, cour_ref)
    fwd, bwd, _ = nums
    p = parity()

    def body(step, carry):
        r, i2 = step // 4, step % 4
        other = 1 - r
        factor = 2.0 * jnp.where(r == 0, fwd[0], bwd[0])

        def load(a, b, c):
            return u_ref[r, :, at(a, b, c)]

        def emit(a, b, c, value):
            s = at(a, b, c)
            z_ref[r, :, s] = value + factor * u_ref[other, :, s]

        stencil(load, emit, i2, nums)
        return carry

    lax.fori_loop(0, 8, body, 0)

    def copy(i, carry):
        s = pl.ds(pl.multiple_of(i * 2048, 2048), 2048)
        near_ref[:, s] = u_ref[p, :, s]
        far_ref[:, s] = u_ref[1 - p, :, s]
        return carry

    lax.fori_loop(0, 8, copy, 0)


def storage_index(packed):
    i2 = packed // 64
    i3 = packed // 32 % 2 * 2 + packed // 4 % 2
    i5 = packed // 8 % 4
    return i2 * 64 + i3 * 16 + packed % 4 * 4 + i5


def point_table(level_ref):
    rows = storage_index(lax.broadcasted_iota(jnp.int32, (256, LANES), 0))
    physical = jnp.zeros((256, LANES), jnp.int32)
    for p in range(4):
        stored = level_ref[0, p] - 2
        physical = physical | (((rows >> (2 * (3 - stored))) & 3) << (2 * (3 - p)))
    halves = []
    for half in range(2):
        cols = storage_index(lax.broadcasted_iota(jnp.int32, (8, LANES), 1) + half * LANES)
        halves.append(jnp.where(physical == cols[0:1], 1.0, 0.0))
    return jnp.concatenate(halves, axis=1).astype(BF16)


def exact_dot(x, table, across):
    high = x.astype(BF16)
    rest = x - high.astype(F32)
    middle = rest.astype(BF16)
    low = (rest - middle.astype(F32)).astype(BF16)
    dims = (((1,), (1 if across else 0,)), ((), ()))
    parts = jnp.concatenate([high, middle, low], axis=0)
    done = lax.dot_general(parts, table, dims, preferred_element_type=F32)
    n = x.shape[0]
    return done[:n] + (done[n : 2 * n] + done[2 * n :])


def second_kernel(
    u_ref,
    z_ref,
    k_ref,
    level_ref,
    diff_ref,
    cour_ref,
    weight_ref,
    acc_ref,
    t_ref,
    own_ref,
    off_ref,
    map_ref,
    full_ref,
):
    nums = numbers(level_ref, diff_ref, cour_ref)
    fwd, bwd, _ = nums
    p = parity()
    q = 1 - p
    _, s_core = sides(fwd, bwd, p)
    twice = 2.0 * fwd[0] * bwd[0]
    square, double = s_core * s_core, 2.0 * s_core
    x = pack(lambda a, b, c: u_ref[p, :, at(a, b, c)])
    y = pack(lambda a, b, c: u_ref[q, :, at(a, b, c)])
    zx = pack(lambda a, b, c: z_ref[p, :, at(a, b, c)])
    off_ref[0:8, :] = double * zx - 3.0 * square * y
    off_ref[8:16, :] = square * x

    def add(i, carry):
        s = pl.ds(pl.multiple_of(i * 2048, 2048), 2048)
        full_ref[q, :, s] = z_ref[q, :, s] + double * k_ref[p, :, s]
        return carry

    lax.fori_loop(0, 8, add, 0)

    def body(step, carry):
        r, i2 = step // 4, step % 4

        def load(a, b, c):
            return full_ref[r, :, at(a, b, c)]

        def emit(a, b, c, value):
            s = at(a, b, c)
            acc_ref[r, :, s] = value + twice * u_ref[r, :, s] + square * k_ref[r, :, s]

        stencil(load, emit, i2, nums)
        return carry

    lax.fori_loop(0, 8, body, 0)
    own_ref[0:8, :] = pack(lambda a, b, c: acc_ref[p, :, at(a, b, c)])
    own_ref[8:16, :] = pack(lambda a, b, c: acc_ref[q, :, at(a, b, c)])
    table = point_table(level_ref)
    map_ref[...] = table
    weight = weight_ref[0].astype(F32)
    both = jnp.concatenate([own_ref[...], off_ref[...]], axis=0)
    t_ref[...] = weight * exact_dot(both, table, False)


def gather_kernel(t_ref, a_ref, b_ref, c_ref, off_ref, far_ref, cross_ref, own_ref):
    total = (t_ref[...] + a_ref[...]) + (b_ref[...] + c_ref[...])
    own_ref[...] = total[0:16]
    cross_ref[...] = total[16:32]
    far_ref[0:16, :] = total[16:32]
    far_ref[16:32, :] = off_ref[...]


def near_kernel(acc_ref, zones_ref, same_ref, level_ref, diff_ref, cour_ref, out_ref, near_ref):
    nums = numbers(level_ref, diff_ref, cour_ref)
    fwd, bwd, _ = nums
    p = parity()
    q = 1 - p
    s_off, _ = sides(fwd, bwd, p)
    square, double = s_off * s_off, 2.0 * s_off

    def gather(i, carry):
        s = pl.ds(pl.multiple_of(i * 2048, 2048), 2048)
        near_ref[:, s] = zones_ref[q, :, s] + same_ref[:, s]
        return carry

    lax.fori_loop(0, 8, gather, 0)

    def body(i2, carry):
        def load(a, b, c):
            return near_ref[:, at(a, b, c)]

        def emit(a, b, c, value):
            s = at(a, b, c)
            out_ref[p, :, s] = acc_ref[p, :, s] + double * value
            out_ref[q, :, s] = acc_ref[q, :, s] + square * near_ref[:, s]

        stencil(load, emit, i2, nums)
        return carry

    lax.fori_loop(0, 4, body, 0)


def change_kernel(acc_ref, own_ref, sum_ref, far_ref, cross_ref, flip_ref, map_ref, out_ref, chunks_ref, wide_ref):
    p = parity()
    total = (sum_ref[...] + flip_ref[...]) + (far_ref[0:16, :] + cross_ref[...])
    own = own_ref[...] + far_ref[16:32, :]
    change = exact_dot(total, map_ref[...], True) - own
    for v, g, j, i2, i3, i4 in spots():
        k = (i2 * 4 + i3) * 4 + i4
        x = change[:, v * LANES : (v + 1) * LANES]
        shift = 32 * g + j
        chunks_ref[k * 16 : (k + 1) * 16, :] = roll(x, LANES - shift, 1) if shift else x
    source = lax.broadcasted_iota(jnp.int32, (LANES, 256), 0)
    target = lax.broadcasted_iota(jnp.int32, (LANES, 256), 1)
    lane = target % LANES
    step = lane // 32
    near = jnp.where(target < LANES, 4 - step, step)
    gap = (lane % 32 - source + 32) % 32
    reach = 8 - jnp.minimum(gap, 32 - gap)
    point = (source % 8 == 0) & (source < 32) & (reach > 0)
    table = jnp.where(point, (near * reach).astype(F32) * (1.0 / 32.0), 0.0).astype(BF16)
    wide_ref[...] = exact_dot(chunks_ref[...], table, False)
    rows = ((0, p), (1, 1 - p))

    def plane(i2, i3, c):
        here = wide_ref[pl.ds(pl.multiple_of((i2 * 16 + i3 * 4 + c) * 16, 16), 16), 0:LANES]
        there = wide_ref[pl.ds(pl.multiple_of((i2 * 16 + i3 * 4 + (c + 1) % 4) * 16, 16), 16), LANES:256]
        return here + there

    def body(i2, carry):
        for c in range(4):
            planes = [plane(i2, i3, c) for i3 in range(4)]
            for d3 in range(8):
                value = planes[d3 // 2]
                if d3 % 2:
                    value = 0.5 * (value + planes[(d3 // 2 + 1) % 4])
                s = at(i2, d3, c)
                for half, r in rows:
                    out_ref[r, :, s] = acc_ref[r, :, s] + value[half * 8 : half * 8 + 8]
        return carry

    lax.fori_loop(0, 4, body, 0)


PARTS = 4


def last_kernel(acc_ref, zones_ref, same_ref, diff_ref, cour_ref, out_ref, row_ref, sems):
    p = parity()
    q = 1 - p
    fwd = [diff_ref[0] - 0.5 * cour_ref[0]]
    bwd = [diff_ref[0] + 0.5 * cour_ref[0]]
    s_off, _ = sides(fwd, bwd, p)
    square = s_off * s_off
    whole_row = pltpu.make_async_copy(acc_ref.at[q], out_ref.at[q], sems.at[PARTS])
    whole_row.start()
    width = COLS // PARTS
    copies = []
    for i in range(PARTS):
        s = pl.ds(i * width, width)
        row_ref[:, s] = acc_ref[p, :, s] + square * (zones_ref[p, :, s] + same_ref[:, s])
        copy = pltpu.make_async_copy(row_ref.at[:, s], out_ref.at[p, :, s], sems.at[i])
        copy.start()
        copies.append(copy)
    whole_row.wait()
    for copy in copies:
        copy.wait()


def call(kernel, outs, spaces, scratch=(), aliases=None, space=VMEM):
    return pl.pallas_call(
        kernel,
        out_shape=[jax.ShapeDtypeStruct(s, d) for s, d in outs],
        in_specs=[pl.BlockSpec(memory_space=m) for m in spaces],
        out_specs=[pl.BlockSpec(memory_space=space) for _ in outs],
        scratch_shapes=list(scratch),
        input_output_aliases=aliases or {},
        compiler_params=pltpu.CompilerParams(vmem_limit_bytes=24 * 2**20),
        cost_estimate=pl.CostEstimate(flops=1000, bytes_accessed=1000, transcendentals=0),
    )


def whole(state_field, level_vectors, combine_weights, diffusion, courant):
    u = state_field[0]
    shape = u.shape
    grids, doms = lax.axis_size("grid"), lax.axis_size("dom")
    pairs_same, pairs_zone = [], []
    for d in range(doms):
        right = (d + 1) % doms
        if d % 2:
            (pairs_same if d % 4 == 1 else pairs_zone).extend([(d, right), (right, d)])
    pairs_off = pairs_same + pairs_zone
    pairs_core = [(d, d ^ 1) for d in range(doms)]
    half = grids // 2
    pairs_flip = [(g, (g + half) % grids) for g in range(grids)]
    pairs_cross = [(g * doms + s, (g + half) % grids * doms + t) for g in range(grids) for s, t in pairs_off]

    numbers_in = (level_vectors, diffusion, courant)
    row, points = (shape[1], shape[2]), (16, 256)
    cores = lax.ppermute(u, "dom", pairs_core)
    zones = lax.ppermute(u, "dom", pairs_zone)
    z, near, far_row = call(first_kernel, [(shape, F32), (row, F32), (row, F32)], [VMEM] + [SMEM] * 3)(u, *numbers_in)
    same_near = lax.ppermute(near, "dom", pairs_same)
    acc, t, own, off, table, _ = call(
        second_kernel,
        [(shape, F32), ((32, 256), F32), (points, F32), (points, F32), ((256, 256), BF16), (shape, F32)],
        [VMEM] * 3 + [SMEM] * 4,
        aliases={1: 5},
    )(u, z, cores, *numbers_in, combine_weights)
    turned = []
    for k in range(1, half):
        pairs = [(g, g // half * half + (g + k) % half) for g in range(grids)]
        turned.append(lax.ppermute(t, "grid", pairs))
    far, cross, total = call(gather_kernel, [((32, 256), F32), (points, F32), (points, F32)], [VMEM] * 5)(
        t, *turned, off
    )
    far_in = lax.ppermute(far, "dom", pairs_off)
    cross_in = lax.ppermute(cross, AXES, pairs_cross)
    flip_in = lax.ppermute(total, "grid", pairs_flip)
    same_far = lax.ppermute(far_row, "dom", pairs_same)
    (acc,) = call(
        near_kernel,
        [(shape, F32)],
        [VMEM] * 3 + [SMEM] * 3,
        scratch=[VMEM(row, F32)],
        aliases={0: 0},
    )(acc, zones, same_near, *numbers_in)
    (acc,) = call(
        change_kernel,
        [(shape, F32)],
        [VMEM] * 7,
        scratch=[VMEM((1024, LANES), F32), VMEM((1024, 256), F32)],
        aliases={0: 0},
    )(acc, own, total, far_in, cross_in, flip_in, table)
    (out,) = call(
        last_kernel,
        [(shape, F32)],
        [VMEM] * 3 + [SMEM] * 2,
        scratch=[VMEM(row, F32), pltpu.SemaphoreType.DMA((PARTS + 1,))],
        space=pl.ANY,
    )(acc, zones, same_far, diffusion, courant)
    return out[None]


def solution(mesh):
    placed = (P("grid", "dom", None, None), P("grid", None), P("grid"), P(), P())
    return jax.shard_map(whole, mesh=mesh, in_specs=placed, out_specs=P("grid", "dom", None, None), check_vma=False)
```

time: 138 us -> 41.7 us (0.30)
  the two profiles are of different devices: /device:TPU:2 before, /device:TPU:24 now
where the time goes in v1:
time: 41.7 us; the launch traced here: 41.5 us
  starting transfers between devices  20.8 us (50%)
  Pallas kernels  11.9 us (29%)
  waiting for transfers between devices  6.76 us (16%)
  local copies, waits for them, and re-layouts  1.25 us (3%)
  between operations  0.78 us (2%)
    ppermute x1, starting transfers between devices, whole(): zones = lax.ppermute(u, 'dom', pairs_zone)  10.3 us
    ppermute x3, waiting for transfers between devices, whole(): turned.append(lax.ppermute(t, 'grid', pairs))  5.48 us
    ppermute x1, starting transfers between devices, whole(): cross_in = lax.ppermute(cross, AXES, pairs_cross)  5.08 us
    ppermute x3, starting transfers between devices, whole(): turned.append(lax.ppermute(t, 'grid', pairs))  3.58 us
    pallas_call x1, Pallas kernels, whole(): call(second_kernel, [(shape, F32), ((32, 256), F32), (points, F32), (poin...  3.57 us
    pallas_call x1, Pallas kernels, whole(): call(first_kernel, [(shape, F32), (row, F32), (row, F32)], [VMEM] + [SMEM...  3 us
    pallas_call x1, Pallas kernels, whole(): call(near_kernel, [(shape, F32)], [VMEM] * 3 + [SMEM] * 3, scratch=[VMEM(...  2.23 us
    pallas_call x1, Pallas kernels, whole(): call(change_kernel, [(shape, F32)], [VMEM] * 7, scratch=[VMEM((1024, LANE...  1.57 us
  transfers between devices with their start and end apart: 10, of which 4 were waited for; matrix products, arithmetic and copies ran while one was open for 0% of the time, Pallas kernels for 25%

profile of v1, /device:TPU:24, one launch (start us, length us, event | category | flops | bytes accessed | tf_op | source)
XLA Modules:
  0.0 41.5 jit_solution(11651153711981007692)
XLA Ops:
  0.0 0.1 collective-permute-start
  0.1 10.3 %collective-permute-start.1 = (f32[2,8,16384]{2,1,0:T(8,128)}, f32[2,8,16384]{2,1,0:T(8,128)S(1)}, u32[]{:S(2)}, u32[]{:S(2)}) collective-permute-start(f32[2,8,16384]{2,1,0:T(8,128)} %bitcast.3), channel_id=1, source_target_pairs={{3,4},{4,3},{7,8},{8,7},{11,12},{12,11},{15,16},{16,15},{19,20},{2... | collective-permute-start | bytes 3145736 | tf_op jit(solution)/shard_map/ppermute | solution.py:355
  10.5 1.2 %copy-done = f32[1,2,8,16384]{3,2,1,0:T(8,128)S(1)} copy-done((f32[1,2,8,16384]{3,2,1,0:T(8,128)S(1)}, f32[1,2,8,16384]{3,2,1,0:T(8,128)}, u32[]{:S(2)}) %copy-start) | copy-done | bytes 1048600
  11.7 3.0 %shard_map.55 = (f32[2,8,16384]{2,1,0:T(8,128)S(1)}, f32[8,16384]{1,0:T(8,128)S(1)}, f32[8,16384]{1,0:T(8,128)S(1)}) custom-call(f32[2,8,16384]{2,1,0:T(8,128)S(1)} %bitcast.4, s32[1,4]{1,0:T(1,128)S(1)} %copy-done.3, f32[6]{0:T(128)S(1)} %copy-done.1, f32[6]{0:T(128)S(1)} %copy-done.2), custom_call_target="tpu_custom_call" | custom-call | flops 1000 | bytes 1000 | tf_op jit(solution)/shard_map/pallas_call | solution.py:356
  14.7 0.7 %collective-permute-start.2 = (f32[8,16384]{1,0:T(8,128)S(1)}, f32[8,16384]{1,0:T(8,128)S(1)}, u32[]{:S(2)}, u32[]{:S(2)}) collective-permute-start(f32[8,16384]{1,0:T(8,128)S(1)} %get-tuple-element.18), channel_id=1, source_target_pairs={{1,2},{2,1},{5,6},{6,5},{9,10},{10,9},{13,14},{14,13},{17,18},{18,... | collective-permute-start | bytes 1572872 | tf_op jit(solution)/shard_map/ppermute | solution.py:357
  15.4 0.7 %collective-permute-start.9 = (f32[8,16384]{1,0:T(8,128)S(1)}, f32[8,16384]{1,0:T(8,128)S(1)}, u32[]{:S(2)}, u32[]{:S(2)}) collective-permute-start(f32[8,16384]{1,0:T(8,128)S(1)} %get-tuple-element.26), channel_id=1, source_target_pairs={{1,2},{2,1},{5,6},{6,5},{9,10},{10,9},{13,14},{14,13},{17,18},{18,... | collective-permute-start | bytes 1572872 | tf_op jit(solution)/shard_map/ppermute | solution.py:374
  16.8 3.6 %shard_map.56 = (f32[2,8,16384]{2,1,0:T(8,128)S(1)}, f32[32,256]{1,0:T(8,128)S(1)}, f32[16,256]{1,0:T(8,128)S(1)}, f32[16,256]{1,0:T(8,128)S(1)}, bf16[256,256]{...) custom-call(f32[2,8,16384]{2,1,0:T(8,128)S(1)} %bitcast.5, ...), custom_call_target="tpu_custom_call", output_to_operand_aliasing={{5}: (1, {})} | custom-call | flops 1000 | bytes 1000 | tf_op jit(solution)/shard_map/pallas_call | solution.py:358
  20.3 0.2 collective-permute-start.3
  20.6 2.6 %collective-permute-start.4 = (f32[32,256]{1,0:T(8,128)S(1)}, f32[32,256]{1,0:T(8,128)S(1)}, u32[]{:S(2)}, u32[]{:S(2)}) collective-permute-start(f32[32,256]{1,0:T(8,128)S(1)} %get-tuple-element.20.t_ref), channel_id=1, source_target_pairs={{0,64},{32,96},{64,0},{96,32},{128,192},{160,224},{192,128},{224,1... | collective-permute-start | bytes 98312 | tf_op jit(solution)/shard_map/ppermute | solution.py:367
  23.2 1.1 %collective-permute-done.3.a_ref = f32[32,256]{1,0:T(8,128)S(1)} collective-permute-done((f32[32,256]{1,0:T(8,128)S(1)}, f32[32,256]{1,0:T(8,128)S(1)}, u32[]{:S(2)}, u32[]{:S(2)}) %collective-permute-start.3) | collective-permute-done | bytes 32800 | tf_op jit(solution)/shard_map/ppermute | solution.py:367
  24.3 0.7 %collective-permute-start.5 = (f32[32,256]{1,0:T(8,128)S(1)}, f32[32,256]{1,0:T(8,128)S(1)}, u32[]{:S(2)}, u32[]{:S(2)}) collective-permute-start(f32[32,256]{1,0:T(8,128)S(1)} %get-tuple-element.20.t_ref), channel_id=1, source_target_pairs={{0,96},{32,0},{64,32},{96,64},{128,224},{160,128},{192,160},{224,1... | collective-permute-start | bytes 98312 | tf_op jit(solution)/shard_map/ppermute | solution.py:367
  25.0 1.0 %collective-permute-done.4.b_ref = f32[32,256]{1,0:T(8,128)S(1)} collective-permute-done((f32[32,256]{1,0:T(8,128)S(1)}, f32[32,256]{1,0:T(8,128)S(1)}, u32[]{:S(2)}, u32[]{:S(2)}) %collective-permute-start.4) | collective-permute-done | bytes 32800 | tf_op jit(solution)/shard_map/ppermute | solution.py:367
  26.0 3.4 %collective-permute-done.5.c_ref = f32[32,256]{1,0:T(8,128)S(1)} collective-permute-done((f32[32,256]{1,0:T(8,128)S(1)}, f32[32,256]{1,0:T(8,128)S(1)}, u32[]{:S(2)}, u32[]{:S(2)}) %collective-permute-start.5) | collective-permute-done | bytes 32800 | tf_op jit(solution)/shard_map/ppermute | solution.py:367
  29.4 0.1 collective-permute-start.6
  29.5 5.1 %collective-permute-start.7 = (f32[16,256]{1,0:T(8,128)S(1)}, f32[16,256]{1,0:T(8,128)S(1)}, u32[]{:S(2)}, u32[]{:S(2)}) collective-permute-start(f32[16,256]{1,0:T(8,128)S(1)} %get-tuple-element.24), channel_id=1, source_target_pairs={{1,130},{2,129},{5,134},{6,133},{9,138},{10,137},{13,142},{14,141}... | collective-permute-start | bytes 49160 | tf_op jit(solution)/shard_map/ppermute | solution.py:372
  34.6 0.0 collective-permute-done.2.same_ref
  34.6 0.2 collective-permute-start.8
  34.8 0.0 collective-permute-done.1.zones_ref
  34.8 2.2 %shard_map.57.acc_ref = f32[2,8,16384]{2,1,0:T(8,128)S(1)} custom-call(f32[2,8,16384]{2,1,0:T(8,128)S(1)} %get-tuple-element.17.acc_ref, f32[2,8,16384]{2,1,0:T(8,128)S(1)} %collective-permute-done.1.zones_ref, f32[8,16384]{1,0:T(8,128)S(1)} %collective-permute-done.2.same_ref, s32[1,4]{1,0:T(1,128)S(1)} %copy-done.3, ...), custom_call_target="tpu_custom_call", output_to_operand_aliasing={{}: (0, {})} | custom-call | flops 1000 | bytes 1000 | tf_op jit(solution)/shard_map/pallas_call | solution.py:375
  37.1 0.0 collective-permute-done.7.cross_ref
  37.1 1.3 %collective-permute-done.8.flip_ref = f32[16,256]{1,0:T(8,128)S(1)} collective-permute-done((f32[16,256]{1,0:T(8,128)S(1)}, f32[16,256]{1,0:T(8,128)S(1)}, u32[]{:S(2)}, u32[]{:S(2)}) %collective-permute-start.8) | collective-permute-done | bytes 16416 | tf_op jit(solution)/shard_map/ppermute | solution.py:373
  38.3 0.0 collective-permute-done.6.far_ref
  38.3 1.6 %shard_map.59.acc_ref = f32[2,8,16384]{2,1,0:T(8,128)S(1)} custom-call(f32[2,8,16384]{2,1,0:T(8,128)S(1)} %shard_map.57.acc_ref, f32[16,256]{1,0:T(8,128)S(1)} %get-tuple-element.19.own_ref, f32[16,256]{1,0:T(8,128)S(1)} %get-tuple-element.22.sum_ref, f32[32,256]{1,0:T(8,128)S(1)} %collective-permute-done.6.far_ref, ...), custom_call_target="tpu_custom_call", output_to_operand_aliasing={{}: (0, {})} | custom-call | flops 1000 | bytes 1000 | tf_op jit(solution)/shard_map/pallas_call | solution.py:382
  39.9 1.6 %shard_map.60 = f32[2,8,16384]{2,1,0:T(8,128)} custom-call(f32[2,8,16384]{2,1,0:T(8,128)S(1)} %shard_map.59.acc_ref, f32[2,8,16384]{2,1,0:T(8,128)S(1)} %collective-permute-done.1.zones_ref, f32[8,16384]{1,0:T(8,128)S(1)} %collective-permute-done.9.same_ref, f32[6]{0:T(128)S(1)} %copy-done.1, f32[6]{0:T(128)S(1)} %copy-done.2), custom_call_target="tpu_custom_call" | custom-call | flops 1000 | bytes 1000 | tf_op jit(solution)/shard_map/pallas_call | solution.py:389
  (10 shorter events, 0.0 us)
Async XLA Ops:
  0.0 10.4 %copy-start.3 = (s32[1,4]{1,0:T(1,128)S(1)}, s32[1,4]{1,0:T(1,128)}, u32[]{:S(2)}) copy-start(s32[1,4]{1,0:T(1,128)} %level_ref.5) | copy-start | bytes 52
  0.0 10.4 %copy-start.1 = (f32[6]{0:T(128)S(1)}, f32[6]{0:T(128)}, u32[]{:S(2)}) copy-start(f32[6]{0:T(128)} %diff_ref.7) | copy-start | bytes 76
  0.0 10.4 %copy-start.2 = (f32[6]{0:T(128)S(1)}, f32[6]{0:T(128)}, u32[]{:S(2)}) copy-start(f32[6]{0:T(128)} %cour_ref.7) | copy-start | bytes 76
  0.0 16.8 %collective-permute-start = (f32[2,8,16384]{2,1,0:T(8,128)}, f32[2,8,16384]{2,1,0:T(8,128)S(1)}, u32[]{:S(2)}, u32[]{:S(2)}) collective-permute-start(f32[2,8,16384]{2,1,0:T(8,128)} %bitcast.2), channel_id=1, source_target_pairs={{0,1},{1,0},{2,3},{3,2},{4,5},{5,4},{6,7},{7,6},{8,9},{9,8},{10,11... | collective-permute-start | bytes 3145736 | tf_op jit(solution)/shard_map/ppermute | solution.py:354
  0.1 34.7 %collective-permute-start.1 = (f32[2,8,16384]{2,1,0:T(8,128)}, f32[2,8,16384]{2,1,0:T(8,128)S(1)}, u32[]{:S(2)}, u32[]{:S(2)}) collective-permute-start(f32[2,8,16384]{2,1,0:T(8,128)} %bitcast.3), channel_id=1, source_target_pairs={{3,4},{4,3},{7,8},{8,7},{11,12},{12,11},{15,16},{16,15},{19,20},{2... | collective-permute-start | bytes 3145736 | tf_op jit(solution)/shard_map/ppermute | solution.py:355
  10.5 1.2 %copy-start = (f32[1,2,8,16384]{3,2,1,0:T(8,128)S(1)}, f32[1,2,8,16384]{3,2,1,0:T(8,128)}, u32[]{:S(2)}) copy-start(f32[1,2,8,16384]{3,2,1,0:T(8,128)} %param.5) | copy-start | bytes 3145732
  14.7 19.9 %collective-permute-start.2 = (f32[8,16384]{1,0:T(8,128)S(1)}, f32[8,16384]{1,0:T(8,128)S(1)}, u32[]{:S(2)}, u32[]{:S(2)}) collective-permute-start(f32[8,16384]{1,0:T(8,128)S(1)} %get-tuple-element.18), channel_id=1, source_target_pairs={{1,2},{2,1},{5,6},{6,5},{9,10},{10,9},{13,14},{14,13},{17,18},{18,... | collective-permute-start | bytes 1572872 | tf_op jit(solution)/shard_map/ppermute | solution.py:357
  15.4 24.5 %collective-permute-start.9 = (f32[8,16384]{1,0:T(8,128)S(1)}, f32[8,16384]{1,0:T(8,128)S(1)}, u32[]{:S(2)}, u32[]{:S(2)}) collective-permute-start(f32[8,16384]{1,0:T(8,128)S(1)} %get-tuple-element.26), channel_id=1, source_target_pairs={{1,2},{2,1},{5,6},{6,5},{9,10},{10,9},{13,14},{14,13},{17,18},{18,... | collective-permute-start | bytes 1572872 | tf_op jit(solution)/shard_map/ppermute | solution.py:374
  20.3 3.9 %collective-permute-start.3 = (f32[32,256]{1,0:T(8,128)S(1)}, f32[32,256]{1,0:T(8,128)S(1)}, u32[]{:S(2)}, u32[]{:S(2)}) collective-permute-start(f32[32,256]{1,0:T(8,128)S(1)} %get-tuple-element.20.t_ref), channel_id=1, source_target_pairs={{0,32},{32,64},{64,96},{96,0},{128,160},{160,192},{192,224},{224,1... | collective-permute-start | bytes 98312 | tf_op jit(solution)/shard_map/ppermute | solution.py:367
  20.6 5.4 %collective-permute-start.4 = (f32[32,256]{1,0:T(8,128)S(1)}, f32[32,256]{1,0:T(8,128)S(1)}, u32[]{:S(2)}, u32[]{:S(2)}) collective-permute-start(f32[32,256]{1,0:T(8,128)S(1)} %get-tuple-element.20.t_ref), channel_id=1, source_target_pairs={{0,64},{32,96},{64,0},{96,32},{128,192},{160,224},{192,128},{224,1... | collective-permute-start | bytes 98312 | tf_op jit(solution)/shard_map/ppermute | solution.py:367
  24.3 5.1 %collective-permute-start.5 = (f32[32,256]{1,0:T(8,128)S(1)}, f32[32,256]{1,0:T(8,128)S(1)}, u32[]{:S(2)}, u32[]{:S(2)}) collective-permute-start(f32[32,256]{1,0:T(8,128)S(1)} %get-tuple-element.20.t_ref), channel_id=1, source_target_pairs={{0,96},{32,0},{64,32},{96,64},{128,224},{160,128},{192,160},{224,1... | collective-permute-start | bytes 98312 | tf_op jit(solution)/shard_map/ppermute | solution.py:367
  29.4 8.9 %collective-permute-start.6 = (f32[32,256]{1,0:T(8,128)S(1)}, f32[32,256]{1,0:T(8,128)S(1)}, u32[]{:S(2)}, u32[]{:S(2)}) collective-permute-start(f32[32,256]{1,0:T(8,128)S(1)} %get-tuple-element.23), channel_id=1, source_target_pairs={{1,2},{2,1},{5,6},{6,5},{9,10},{10,9},{13,14},{14,13},{17,18},{18,... | collective-permute-start | bytes 98312 | tf_op jit(solution)/shard_map/ppermute | solution.py:371
  29.5 7.6 %collective-permute-start.7 = (f32[16,256]{1,0:T(8,128)S(1)}, f32[16,256]{1,0:T(8,128)S(1)}, u32[]{:S(2)}, u32[]{:S(2)}) collective-permute-start(f32[16,256]{1,0:T(8,128)S(1)} %get-tuple-element.24), channel_id=1, source_target_pairs={{1,130},{2,129},{5,134},{6,133},{9,138},{10,137},{13,142},{14,141}... | collective-permute-start | bytes 49160 | tf_op jit(solution)/shard_map/ppermute | solution.py:372
  34.6 3.7 %collective-permute-start.8 = (f32[16,256]{1,0:T(8,128)S(1)}, f32[16,256]{1,0:T(8,128)S(1)}, u32[]{:S(2)}, u32[]{:S(2)}) collective-permute-start(f32[16,256]{1,0:T(8,128)S(1)} %get-tuple-element.22.sum_ref), channel_id=1, source_target_pairs={{0,128},{32,160},{64,192},{96,224},{128,0},{160,32},{192,64},{224,... | collective-permute-start | bytes 49160 | tf_op jit(solution)/shard_map/ppermute | solution.py:373
